TPU v7x, 32 devices: a whole 2x2x4 slice. The times are simulated.
32 devices in a mesh: fsdp: 8 (over z, x), tensor: 2 (over y), dp: 2 (over core).
Axes of the slice: x: 2, y: 2, z: 4, core: 2. Of those that a mesh axis runs over, the one named last changes fastest.
Arguments:
- states: bfloat16 [4096, 4096], P('fsdp', ('tensor', 'dp')), may hold values from -6 to 6
- fresh_rows: bfloat16 [4096, 4096], P('fsdp', ('tensor', 'dp')), may hold values from -6 to 6
- norm_gain: bfloat16 [4096], P(('tensor', 'dp')), may hold values from 0.25 to 1.75
- gate_weight: bfloat16 [4096, 8192], P('fsdp', ('tensor', 'dp')), may hold values from -0.09375 to 0.09375
- up_weight: bfloat16 [4096, 8192], P('fsdp', ('tensor', 'dp')), may hold values from -0.09375 to 0.09375
- down_weight: bfloat16 [8192, 4096], P(('tensor', 'dp'), 'fsdp'), may hold values from -0.09375 to 0.09375
- halted: int32 [64, 64], P('fsdp'), may hold values from 0 to 1, as said below
- refill_index: int32 [64, 64], P('fsdp'), may hold values from 0 to 63, each once within a row
Outputs:
- next_states: bfloat16 [4096, 4096], P('fsdp', ('tensor', 'dp'))
Inputs may be any that keep to these rules, and one draw needn't show every extreme that they name: In each aligned block of 512 rows (in row order over all batches) at most 384 rows are running (halted 0), and some block has exactly 384 running rows. Each batch's row of refill_index holds every number of 0 to 63 once.
All inputs are finite; a program needn't handle non-finite values.
Results may differ from a plain program's by a relative error of at most 0.0085.
Values may be sent and summed in bfloat16 or wider, within the bound.
A program may use at most 128 MiB of HBM per device.

v0:
```python
import jax
import jax.numpy as jnp
from jax import lax
from jax.sharding import PartitionSpec as P

norm_eps = 1e-05


def block_update(source, norm_gain, gate_weight, up_weight, down_weight):
    gathered, gain_full = (
        lax.all_gather(source, ("tensor", "dp"), axis=1, tiled=True),
        lax.all_gather(norm_gain, ("tensor", "dp"), axis=0, tiled=True),
    )
    widened = gathered.astype(jnp.float32)
    mean_square = jnp.mean(widened * widened, axis=-1, keepdims=True)
    normed = (widened * lax.rsqrt(mean_square + norm_eps) * gain_full.astype(jnp.float32)).astype(
        jnp.bfloat16
    )
    gate_more = jnp.dot(
        normed,
        lax.all_gather(gate_weight, "fsdp", axis=0, tiled=True),
        preferred_element_type=jnp.float32,
    )
    up_more = jnp.dot(
        normed,
        lax.all_gather(up_weight, "fsdp", axis=0, tiled=True),
        preferred_element_type=jnp.float32,
    )
    hidden = (jax.nn.silu(gate_more) * up_more).astype(jnp.bfloat16)
    partial_value = jnp.dot(
        hidden,
        lax.all_gather(down_weight, "fsdp", axis=1, tiled=True),
        preferred_element_type=jnp.float32,
    )
    return lax.psum_scatter(
        partial_value.astype(jnp.bfloat16), ("tensor", "dp"), scatter_dimension=1, tiled=True
    ).astype(jnp.float32)


def body(states, fresh_rows, norm_gain, gate_weight, up_weight, down_weight, halted, refill_index):
    row_count = states.shape[0]
    running = halted.reshape(row_count) == 0
    capacity = row_count * 3 // 4
    slot_of = jnp.cumsum(running.astype(jnp.int32)) - 1
    slot_ids = lax.iota(jnp.int32, capacity)
    picker = ((slot_of[None, :] == slot_ids[:, None]) & running[None, :]).astype(jnp.bfloat16)
    source = jnp.dot(picker, states, preferred_element_type=jnp.float32).astype(jnp.bfloat16)
    compact = block_update(source, norm_gain, gate_weight, up_weight, down_weight)
    update = jnp.take(compact, jnp.clip(slot_of, 0, capacity - 1), axis=0)
    block_total = refill_index.shape[0]
    batch_len = refill_index.shape[1]
    fresh_blocks = fresh_rows.reshape(block_total, batch_len, fresh_rows.shape[1])
    refilled = jax.vmap(lambda block_rows, pick_index: block_rows[pick_index])(
        fresh_blocks, refill_index
    )
    refilled = refilled.reshape(row_count, fresh_rows.shape[1])
    computed = (states.astype(jnp.float32) + update).astype(jnp.bfloat16)
    return jnp.where(running[:, None], computed, refilled)


def solution(mesh):
    in_specs = (
        P("fsdp", ("tensor", "dp")),
        P("fsdp", ("tensor", "dp")),
        P(("tensor", "dp")),
        P("fsdp", ("tensor", "dp")),
        P("fsdp", ("tensor", "dp")),
        P(("tensor", "dp"), "fsdp"),
        P("fsdp", None),
        P("fsdp", None),
    )
    out_specs = P("fsdp", ("tensor", "dp"))
    return jax.shard_map(body, mesh=mesh, in_specs=in_specs, out_specs=out_specs, check_vma=False)
```

profile of v0, /device:TPU:0, one launch (start us, length us, event | category | flops | bytes accessed | tf_op | source)
XLA Modules:
  0.0 803.4 jit_solution(10444308348933228802)
XLA Ops:
  6.5 0.0 copy-start
  6.5 0.0 all-gather.5.cloned.1.call-start
  6.5 0.8 fusion.21
  7.3 0.1 reshape.107
  7.4 0.3 reduce-window.9
  7.7 0.1 slice.7
  7.8 0.1 slice_reduce_fusion
  7.9 0.1 compare_and_fusion
  8.0 0.1 eq.40
  8.1 2.7 convolution_convert_fusion.1
  10.8 0.0 all-gather.5.cloned.1.call-update
  10.8 0.0 copy-start.2
  10.8 0.0 all-gather.7.cloned.1.call-start
  10.9 0.7 all-gather.7.cloned.1.call-update
  11.6 0.0 all-gather.11.cloned.1.call-start
  11.6 0.7 all-gather.11.cloned.1.call-update
  12.3 0.0 all-gather.9.cloned.1.call-start
  12.4 0.5 all-gather.9.cloned.1.call-update
  12.9 0.0 reduce-scatter.2.cloned.1.call-start
  12.9 0.0 copy-done.2
  12.9 6.2 all_gather.16
  19.1 23.1 %all-gather.5.cloned.1.call-done = bf16[384,4096]{1,0:T(8,128)(2,1)} async-done(((bf16[384,1024]{1,0:T(8,128)(2,1)}), bf16[384,4096]{1,0:T(8,128)(2,1)}) %all-gather.5.cloned.1.call-update) | async-done | bytes 3145744 | tf_op jit(solution)/shard_map/all_gather | solution.py:11
  42.2 2.6 fusion
  44.8 226.8 %all-gather.7.cloned.1.call-done = bf16[4096,2048]{1,0:T(8,128)(2,1)} async-done(((bf16[512,2048]{1,0:T(8,128)(2,1)}), bf16[4096,2048]{1,0:T(8,128)(2,1)}) %all-gather.7.cloned.1.call-update) | async-done | bytes 16777232 | tf_op jit(solution)/shard_map/all_gather | solution.py:21
  271.6 12.3 %fusion.7 = f32[384,2048]{1,0:T(8,128)} fusion(bf16[4096,2048]{1,0:T(8,128)(2,1)} %all-gather.7.cloned.1.call-done, bf16[384,4096]{1,0:T(8,128)(2,1)} %all-gather.5.cloned.1.call-done, f32[4096]{0:T(1024)S(1)} %convert_element_type.40, f32[384]{0:T(512)S(1)} %add_rsqrt_fusion), kind=kOutput, calls=%fused_computation.13 | convolution fusion | flops 6448742400 | bytes 23086592 | tf_op jit(solution)/shard_map/dot_general | solution.py:19
  284.0 215.2 %all-gather.11.cloned.1.call-done = bf16[2048,4096]{1,0:T(8,128)(2,1)} async-done(((bf16[2048,512]{1,0:T(8,128)(2,1)}), bf16[2048,4096]{1,0:T(8,128)(2,1)}) %all-gather.11.cloned.1.call-update) | async-done | bytes 16777232 | tf_op jit(solution)/shard_map/all_gather | solution.py:32
  499.2 227.5 %all-gather.9.cloned.1.call-done = bf16[4096,2048]{1,0:T(8,128)(2,1)} async-done(((bf16[512,2048]{1,0:T(8,128)(2,1)}), bf16[4096,2048]{1,0:T(8,128)(2,1)}) %all-gather.9.cloned.1.call-update) | async-done | bytes 16777232 | tf_op jit(solution)/shard_map/all_gather | solution.py:26
  726.7 26.5 %convolution_convert_fusion = bf16[384,4096]{1,0:T(8,128)(2,1)} fusion(bf16[2048,4096]{1,0:T(8,128)(2,1)} %all-gather.11.cloned.1.call-done, f32[384,2048]{1,0:T(8,128)} %fusion.7, bf16[4096,2048]{1,0:T(8,128)(2,1)} %all-gather.9.cloned.1.call-done, bf16[384,4096]{1,0:T(8,128)(2,1)} %all-gather.5.cloned.1.call-done, f32[4096]{0:T(1024)S(1)} %convert_element_type.40, ...), kind=kOutput, calls=%fused_computation.7 | convolution fusion | flops 12897484800 | bytes 43009536 | tf_op jit(solution)/shard_map/dot_general | solution.py:30
  753.2 0.0 copy-start.1
  753.2 0.0 reduce-scatter.2.cloned.1.call-update
  753.2 0.7 copy-done.1
  753.9 0.1 reshape.116
  753.9 0.0 copy-done
  754.0 7.9 gather_fusion.1
  761.9 0.1 fusion.17
  762.0 27.3 %reduce-scatter.2.cloned.1.call-done = bf16[384,1024]{1,0:T(8,128)(2,1)} async-done(((bf16[384,4096]{1,0:T(8,128)(2,1)}), bf16[384,1024]{1,0:T(8,128)(2,1)}) %reduce-scatter.2.cloned.1.call-update) | async-done | bytes 786448 | tf_op jit(solution)/shard_map/reduce_scatter | solution.py:35
  789.3 1.3 convert_element_type.44
  790.6 2.7 gather_fusion
  793.3 3.6 fusion.4
  (6 shorter events, 0.1 us)
Async XLA Ops:
  6.5 747.4 %copy-start = (bf16[512,1024]{1,0:T(8,128)(2,1)S(1)}, bf16[512,1024]{1,0:T(8,128)(2,1)}, u32[]{:S(2)}) copy-start(bf16[512,1024]{1,0:T(8,128)(2,1)} %param.9) | copy-start | bytes 3145732
  6.5 35.7 %all-gather.5.cloned.1.call-start = ((), (), s32[]{:S(2)}) async-start(), calls=%async_computation.1 | async-start | bytes 3932160 | tf_op jit(solution)/shard_map/all_gather | solution.py:11
  10.8 2.1 copy-start.2
  10.8 260.8 %all-gather.7.cloned.1.call-start = ((), (), s32[]{:S(2)}) async-start(), calls=%async_computation.2 | async-start | bytes 18874368 | tf_op jit(solution)/shard_map/all_gather | solution.py:21
  11.6 487.6 %all-gather.11.cloned.1.call-start = ((), (), s32[]{:S(2)}) async-start(), calls=%async_computation.4 | async-start | bytes 18874368 | tf_op jit(solution)/shard_map/all_gather | solution.py:32
  12.3 714.4 %all-gather.9.cloned.1.call-start = ((), (), s32[]{:S(2)}) async-start(), calls=%async_computation.3 | async-start | bytes 18874368 | tf_op jit(solution)/shard_map/all_gather | solution.py:26
  12.9 776.4 %reduce-scatter.2.cloned.1.call-start = ((), (), s32[]{:S(2)}) async-start(), calls=%async_computation.5 | async-start | bytes 3932160 | tf_op jit(solution)/shard_map/reduce_scatter | solution.py:35
  753.2 0.7 copy-start.1
Sparse Core Ops, SparseCore 0:
  10.9 31.2 all-gather.4
  44.3 227.2 all-gather.6
  273.7 225.4 all-gather.10
  501.2 225.4 all-gather.8
  753.3 35.9 reduce-scatter.1
where the time goes:
time: 804 us; the launch traced here: 803 us
  waiting for transfers between devices  722 us (90%)
  matrix products  41.5 us (5%)
  between operations  13.2 us (2%)
  local copies, waits for them, and re-layouts  11.7 us (1%)
  other arithmetic  8.79 us (1%)
    all_gather x1, waiting for transfers between devices, block_update(): lax.all_gather(up_weight, 'fsdp', axis=0, tiled=True)  227 us
    all_gather x1, waiting for transfers between devices, block_update(): lax.all_gather(gate_weight, 'fsdp', axis=0, tiled=True)  227 us
    all_gather x1, waiting for transfers between devices, block_update(): lax.all_gather(down_weight, 'fsdp', axis=1, tiled=True)  215 us
    reduce_scatter x1, waiting for transfers between devices, block_update(): lax.psum_scatter(partial_value.astype(jnp.bfloat16), ('tensor', 'dp'), sc...  27.3 us
    dot_general x1, matrix products, block_update(): jnp.dot(hidden, lax.all_gather(down_weight, 'fsdp', axis=1, tiled=True),...  26.5 us
    all_gather x1, waiting for transfers between devices, block_update(): lax.all_gather(source, ('tensor', 'dp'), axis=1, tiled=True)  23.1 us
  transfers between devices with their start and end apart: 5, of which 5 were waited for; matrix products, arithmetic and copies ran while one was open for 3% of the time, Pallas kernels for 0%

commit v1 on v0

--- a/solution.py
+++ b/solution.py
@@ -1,9 +1,42 @@
+import functools
 import jax
 import jax.numpy as jnp
 from jax import lax
 from jax.sharding import PartitionSpec as P
 
 norm_eps = 1e-05
+
+
+def plan_patch(x_part, along_axis, in_dim):
+    piece_out = lax.psum(1, along_axis)
+    heard = lax.axis_index(along_axis)
+    block_last, y2, field_out = (piece_out, heard, x_part.shape[in_dim])
+    in_order = []
+    for c, j in enumerate(x_part.shape):
+        in_order.append(j * block_last if c == in_dim else j)
+    mixed_arr = jnp.zeros(in_order, x_part.dtype)
+    mat_out = lax.dynamic_update_slice_in_dim(mixed_arr, x_part, y2 * field_out, axis=in_dim)
+    met_up = work_now = x_part
+    for it in range(1, block_last // 2 + 1):
+        heap = []
+        for c in range(block_last):
+            heap.append((c, (c + 1) % block_last))
+        met_up = lax.ppermute(met_up, axis_name=along_axis, perm=heap)
+        mat_out = lax.dynamic_update_slice_in_dim(
+            mat_out, met_up, (y2 - it) % block_last * field_out, axis=in_dim
+        )
+        if 2 * it < block_last:
+            sides = []
+            for c in range(block_last):
+                sides.append((c, (c - 1) % block_last))
+            work_now = lax.ppermute(work_now, axis_name=along_axis, perm=sides)
+            mat_out = lax.dynamic_update_slice_in_dim(
+                mat_out, work_now, (y2 + it) % block_last * field_out, axis=in_dim
+            )
+    return mat_out
+
+
+name_the_packet = functools.partial(plan_patch, along_axis="fsdp", in_dim=0)
 
 
 def block_update(source, norm_gain, gate_weight, up_weight, down_weight):
@@ -16,11 +49,7 @@
     normed = (widened * lax.rsqrt(mean_square + norm_eps) * gain_full.astype(jnp.float32)).astype(
         jnp.bfloat16
     )
-    gate_more = jnp.dot(
-        normed,
-        lax.all_gather(gate_weight, "fsdp", axis=0, tiled=True),
-        preferred_element_type=jnp.float32,
-    )
+    gate_more = jnp.dot(normed, name_the_packet(gate_weight), preferred_element_type=jnp.float32)
     up_more = jnp.dot(
         normed,
         lax.all_gather(up_weight, "fsdp", axis=0, tiled=True),

time: 804 us -> 789 us (0.981)
  waiting for transfers between devices: 722 us -> 647 us
  starting transfers between devices: 0.16 us -> 34.8 us
  local copies, waits for them, and re-layouts: 11.7 us -> 38.2 us
    ppermute x0 -> x7, waiting for transfers between devices: none -> 399 us  [the longest x4 399 us: plan_patch(): met_up = lax.ppermute(met_up, axis_name=along_axis, perm=heap)]
    all_gather x1, waiting for transfers between devices: 227 us -> 0.01 us  [block_update(): lax.all_gather(up_weight, 'fsdp', axis=0, tiled=True)]
    all_gather x1 -> x0, waiting for transfers between devices: 227 us -> none  [block_update(): lax.all_gather(gate_weight, 'fsdp', axis=0, tiled=True)]
    ppermute x0 -> x7, starting transfers between devices: none -> 34.7 us  [the longest x3 24.1 us: plan_patch(): work_now = lax.ppermute(work_now, axis_name=along_axis, perm=sides)]
    all_gather x1, waiting for transfers between devices: 23.1 us -> 0.01 us  [block_update(): lax.all_gather(source, ('tensor', 'dp'), axis=1, tiled=True)]
    dynamic_update_slice x0 -> x8, local copies, waits for them, and re-layouts: none -> 20.5 us  [the longest x3 9.54 us: plan_patch(): lax.dynamic_update_slice_in_dim(mat_out, work_now, (y2 + it) % block_last...]
  transfers between devices with their start and end apart: 5 -> 11, of which waited for: 5 -> 6; matrix products, arithmetic and copies ran while one was open for 3% -> 6% of each run, Pallas kernels for 0% -> 0%
where the time goes in v1:
time: 789 us
  waiting for transfers between devices  647 us (82%)
  matrix products  41.6 us (5%)
  local copies, waits for them, and re-layouts  38.2 us (5%)
  starting transfers between devices  34.8 us (4%)
  between operations  13.2 us (2%)
  other arithmetic  8.8 us (1%)
    ppermute x4, waiting for transfers between devices, plan_patch(): met_up = lax.ppermute(met_up, axis_name=along_axis, perm=heap)  399 us
    all_gather x1, waiting for transfers between devices, block_update(): lax.all_gather(down_weight, 'fsdp', axis=1, tiled=True)  220 us
    reduce_scatter x1, waiting for transfers between devices, block_update(): lax.psum_scatter(partial_value.astype(jnp.bfloat16), ('tensor', 'dp'), sc...  27.3 us
    dot_general x1, matrix products, block_update(): jnp.dot(hidden, lax.all_gather(down_weight, 'fsdp', axis=1, tiled=True),...  26.3 us
    ppermute x3, starting transfers between devices, plan_patch(): work_now = lax.ppermute(work_now, axis_name=along_axis, perm=sides)  24.1 us
  transfers between devices with their start and end apart: 11, of which 6 were waited for; matrix products, arithmetic and copies ran while one was open for 6% of the time, Pallas kernels for 0%

profile of v1, /device:TPU:0, one launch (start us, length us, event | category | flops | bytes accessed | tf_op | source)
XLA Modules:
  0.0 789.0 jit_solution(4637743029943535541)
XLA Ops:
  6.5 0.8 fusion.25
  7.3 0.1 reshape.107
  7.4 0.3 reduce-window.9
  7.7 0.1 slice.7
  7.8 0.1 slice_reduce_fusion
  7.9 0.1 compare_and_fusion
  8.0 0.1 eq.48
  8.1 2.8 convolution_convert_fusion.1
  10.9 0.0 all-gather.4.cloned.1.call-update
  11.0 0.0 all-gather.6.cloned.1.call-start
  11.0 0.7 all-gather.6.cloned.1.call-update
  11.7 0.0 all-gather.8.cloned.1.call-start
  11.8 0.7 all-gather.8.cloned.1.call-update
  12.5 0.0 reduce-scatter.2.cloned.1.call-start
  12.5 3.0 collective-permute-start
  15.5 3.1 collective-permute-start.1
  18.6 109.2 %collective-permute-done = bf16[512,2048]{1,0:T(8,128)(2,1)S(1)} collective-permute-done((bf16[512,2048]{1,0:T(8,128)(2,1)S(1)}, bf16[512,2048]{1,0:T(8,128)(2,1)S(1)}, u32[]{:S(2)}, u32[]{:S(2)}) %collective-permute-start) | collective-permute-done | bytes 2097184 | tf_op jit(solution)/shard_map/ppermute | solution.py:24
  127.8 2.5 collective-permute-start.2
  130.3 4.3 collective-permute-start.3
  134.7 124.7 %collective-permute-done.2 = bf16[512,2048]{1,0:T(8,128)(2,1)} collective-permute-done((bf16[512,2048]{1,0:T(8,128)(2,1)S(1)}, bf16[512,2048]{1,0:T(8,128)(2,1)}, u32[]{:S(2)}, u32[]{:S(2)}) %collective-permute-start.2) | collective-permute-done | bytes 2097184 | tf_op jit(solution)/shard_map/ppermute | solution.py:24
  259.4 2.6 collective-permute-start.4
  261.9 5.2 all_gather.13
  267.1 16.6 %collective-permute-start.5 = (bf16[512,2048]{1,0:T(8,128)(2,1)}, bf16[512,2048]{1,0:T(8,128)(2,1)}, u32[]{:S(2)}, u32[]{:S(2)}) collective-permute-start(bf16[512,2048]{1,0:T(8,128)(2,1)} %collective-permute-done.3), channel_id=1, source_target_pairs={{0,28},{4,0},{8,4},{12,8},{16,12},{20,16},{24,20},{28,24},{1,29},{... | collective-permute-start | bytes 6291464 | tf_op jit(solution)/shard_map/ppermute | solution.py:32
  283.8 6.0 broadcast_in_dim.32
  289.8 1.6 constant_dynamic-update-slice_fusion.7
  291.3 105.8 %collective-permute-done.4 = bf16[512,2048]{1,0:T(8,128)(2,1)} collective-permute-done((bf16[512,2048]{1,0:T(8,128)(2,1)}, bf16[512,2048]{1,0:T(8,128)(2,1)}, u32[]{:S(2)}, u32[]{:S(2)}) %collective-permute-start.4) | collective-permute-done | bytes 2097184 | tf_op jit(solution)/shard_map/ppermute | solution.py:24
  397.2 2.5 collective-permute-start.6
  399.6 1.4 constant_dynamic-update-slice_fusion.6
  401.1 3.2 constant_dynamic-update-slice_fusion.5
  404.3 3.2 constant_dynamic-update-slice_fusion.4
  407.5 3.1 constant_dynamic-update-slice_fusion.3
  410.6 2.6 fusion
  413.2 3.2 constant_dynamic-update-slice_fusion.2
  416.4 3.2 constant_dynamic-update-slice_fusion.1
  419.6 59.4 %collective-permute-done.6 = bf16[512,2048]{1,0:T(8,128)(2,1)S(1)} collective-permute-done((bf16[512,2048]{1,0:T(8,128)(2,1)}, bf16[512,2048]{1,0:T(8,128)(2,1)S(1)}, u32[]{:S(2)}, u32[]{:S(2)}) %collective-permute-start.6) | collective-permute-done | bytes 2097184 | tf_op jit(solution)/shard_map/ppermute | solution.py:24
  478.9 1.6 constant_dynamic-update-slice_fusion
  480.6 12.4 %fusion.5 = f32[384,2048]{1,0:T(8,128)} fusion(bf16[4096,2048]{1,0:T(8,128)(2,1)} %all-gather.6.cloned.1.call-done, bf16[384,4096]{1,0:T(8,128)(2,1)} %all-gather.4.cloned.1.call-done, f32[4096]{0:T(1024)S(1)} %convert_element_type.40, f32[384]{0:T(512)S(1)} %add_rsqrt_fusion), kind=kOutput, calls=%fused_computation.13 | convolution fusion | flops 6448742400 | bytes 23086592 | tf_op jit(solution)/shard_map/dot_general | solution.py:53
  493.0 219.5 %all-gather.8.cloned.1.call-done = bf16[2048,4096]{1,0:T(8,128)(2,1)} async-done(((bf16[2048,512]{1,0:T(8,128)(2,1)}), bf16[2048,4096]{1,0:T(8,128)(2,1)}) %all-gather.8.cloned.1.call-update) | async-done | bytes 16777232 | tf_op jit(solution)/shard_map/all_gather | solution.py:61
  712.5 26.3 %convolution_convert_fusion = bf16[384,4096]{1,0:T(8,128)(2,1)} fusion(bf16[2048,4096]{1,0:T(8,128)(2,1)} %all-gather.8.cloned.1.call-done, f32[384,2048]{1,0:T(8,128)} %fusion.5, bf16[4096,2048]{1,0:T(8,128)(2,1)} %constant_dynamic-update-slice_fusion, bf16[384,4096]{1,0:T(8,128)(2,1)} %all-gather.4.cloned.1.call-done, f32[4096]{0:T(1024)S(1)} %convert_element_type.40, ...), kind=kOutput, calls=%fused_computation.7 | convolution fusion | flops 12897484800 | bytes 43009536 | tf_op jit(solution)/shard_map/dot_general | solution.py:59
  738.8 0.0 reduce-scatter.2.cloned.1.call-update
  738.8 0.7 copy-done.4
  739.5 0.1 reshape.116
  739.6 7.9 %gather_fusion.1 = bf16[512,1024]{1,0:T(8,128)(2,1)} fusion(bf16[8,64,1024]{2,1,0:T(8,128)(2,1)S(1)} %bitcast.16, s32[512]{0:T(512)S(1)} %reshape.116), kind=kCustom, calls=%fused_computation.1 | custom fusion | bytes 2101248 | tf_op jit(solution)/shard_map/vmap()/gather | solution.py:82
  747.5 0.1 fusion.21
  747.6 27.3 %reduce-scatter.2.cloned.1.call-done = bf16[384,1024]{1,0:T(8,128)(2,1)} async-done(((bf16[384,4096]{1,0:T(8,128)(2,1)}), bf16[384,1024]{1,0:T(8,128)(2,1)}) %reduce-scatter.2.cloned.1.call-update) | async-done | bytes 786448 | tf_op jit(solution)/shard_map/reduce_scatter | solution.py:64
  774.9 1.3 convert_element_type.44
  776.2 2.7 gather_fusion
  778.9 3.6 fusion.4
  (23 shorter events, 0.1 us)
Async XLA Ops:
  6.5 733.0 %copy-start = (bf16[512,1024]{1,0:T(8,128)(2,1)S(1)}, bf16[512,1024]{1,0:T(8,128)(2,1)}, u32[]{:S(2)}) copy-start(bf16[512,1024]{1,0:T(8,128)(2,1)} %param.9) | copy-start | bytes 3145732
  6.5 404.1 %all-gather.4.cloned.1.call-start = ((), (), s32[]{:S(2)}) async-start(), calls=%async_computation.1 | async-start | bytes 3932160 | tf_op jit(solution)/shard_map/all_gather | solution.py:44
  8.1 4.4 copy-start.1
  10.9 251.0 %copy-start.5 = (bf16[1024]{0:T(1024)(128)(2,1)S(1)}, bf16[1024]{0:T(1024)(128)(2,1)}, u32[]{:S(2)}) copy-start(bf16[1024]{0:T(1024)(128)(2,1)} %param.10) | copy-start | bytes 6148
  11.0 469.6 %all-gather.6.cloned.1.call-start = ((), (), s32[]{:S(2)}) async-start(), calls=%async_computation.2 | async-start | bytes 18874368 | tf_op jit(solution)/shard_map/all_gather | solution.py:55
  11.7 700.8 %all-gather.8.cloned.1.call-start = ((), (), s32[]{:S(2)}) async-start(), calls=%async_computation.3 | async-start | bytes 18874368 | tf_op jit(solution)/shard_map/all_gather | solution.py:61
  12.5 762.4 %reduce-scatter.2.cloned.1.call-start = ((), (), s32[]{:S(2)}) async-start(), calls=%async_computation.4 | async-start | bytes 3932160 | tf_op jit(solution)/shard_map/reduce_scatter | solution.py:64
  12.5 115.3 %collective-permute-start = (bf16[512,2048]{1,0:T(8,128)(2,1)S(1)}, bf16[512,2048]{1,0:T(8,128)(2,1)S(1)}, u32[]{:S(2)}, u32[]{:S(2)}) collective-permute-start(bf16[512,2048]{1,0:T(8,128)(2,1)S(1)} %copy-done.1), channel_id=1, source_target_pairs={{0,4},{4,8},{8,12},{12,16},{16,20},{20,24},{24,28},{28,0},{1,5},{5... | collective-permute-start | bytes 6291464 | tf_op jit(solution)/shard_map/ppermute | solution.py:24
  15.5 114.8 %collective-permute-start.1 = (bf16[512,2048]{1,0:T(8,128)(2,1)S(1)}, bf16[512,2048]{1,0:T(8,128)(2,1)}, u32[]{:S(2)}, u32[]{:S(2)}) collective-permute-start(bf16[512,2048]{1,0:T(8,128)(2,1)S(1)} %copy-done.1), channel_id=1, source_target_pairs={{0,28},{4,0},{8,4},{12,8},{16,12},{20,16},{24,20},{28,24},{1,29},{... | collective-permute-start | bytes 6291464 | tf_op jit(solution)/shard_map/ppermute | solution.py:32
  127.8 2.5 copy-start.2
  127.8 131.5 %collective-permute-start.2 = (bf16[512,2048]{1,0:T(8,128)(2,1)S(1)}, bf16[512,2048]{1,0:T(8,128)(2,1)}, u32[]{:S(2)}, u32[]{:S(2)}) collective-permute-start(bf16[512,2048]{1,0:T(8,128)(2,1)S(1)} %collective-permute-done), channel_id=1, source_target_pairs={{0,4},{4,8},{8,12},{12,16},{16,20},{20,24},{24,28},{28,0},{1,5},{5... | collective-permute-start | bytes 6291464 | tf_op jit(solution)/shard_map/ppermute | solution.py:24
  130.3 136.8 %collective-permute-start.3 = (bf16[512,2048]{1,0:T(8,128)(2,1)}, bf16[512,2048]{1,0:T(8,128)(2,1)}, u32[]{:S(2)}, u32[]{:S(2)}) collective-permute-start(bf16[512,2048]{1,0:T(8,128)(2,1)} %collective-permute-done.1), channel_id=1, source_target_pairs={{0,28},{4,0},{8,4},{12,8},{16,12},{20,16},{24,20},{28,24},{1,29},{... | collective-permute-start | bytes 6291464 | tf_op jit(solution)/shard_map/ppermute | solution.py:32
  259.4 137.8 %collective-permute-start.4 = (bf16[512,2048]{1,0:T(8,128)(2,1)}, bf16[512,2048]{1,0:T(8,128)(2,1)}, u32[]{:S(2)}, u32[]{:S(2)}) collective-permute-start(bf16[512,2048]{1,0:T(8,128)(2,1)} %collective-permute-done.2), channel_id=1, source_target_pairs={{0,4},{4,8},{8,12},{12,16},{16,20},{20,24},{24,28},{28,0},{1,5},{5... | collective-permute-start | bytes 6291464 | tf_op jit(solution)/shard_map/ppermute | solution.py:24
  267.1 149.3 %collective-permute-start.5 = (bf16[512,2048]{1,0:T(8,128)(2,1)}, bf16[512,2048]{1,0:T(8,128)(2,1)}, u32[]{:S(2)}, u32[]{:S(2)}) collective-permute-start(bf16[512,2048]{1,0:T(8,128)(2,1)} %collective-permute-done.3), channel_id=1, source_target_pairs={{0,28},{4,0},{8,4},{12,8},{16,12},{20,16},{24,20},{28,24},{1,29},{... | collective-permute-start | bytes 6291464 | tf_op jit(solution)/shard_map/ppermute | solution.py:32
  289.8 109.9 %copy-start.3 = (bf16[512,2048]{1,0:T(8,128)(2,1)S(1)}, bf16[512,2048]{1,0:T(8,128)(2,1)}, u32[]{:S(2)}) copy-start(bf16[512,2048]{1,0:T(8,128)(2,1)} %copy-done.2) | copy-start | bytes 6291460
  397.2 81.8 %collective-permute-start.6 = (bf16[512,2048]{1,0:T(8,128)(2,1)}, bf16[512,2048]{1,0:T(8,128)(2,1)S(1)}, u32[]{:S(2)}, u32[]{:S(2)}) collective-permute-start(bf16[512,2048]{1,0:T(8,128)(2,1)} %collective-permute-done.4), channel_id=1, source_target_pairs={{0,4},{4,8},{8,12},{12,16},{16,20},{20,24},{24,28},{28,0},{1,5},{5... | collective-permute-start | bytes 6291464 | tf_op jit(solution)/shard_map/ppermute | solution.py:24
  738.8 0.7 copy-start.4
Sparse Core Ops, SparseCore 0:
  11.1 31.2 all-gather.3
  44.5 424.0 all-gather.5
  470.6 241.8 all-gather.7
  739.0 35.8 reduce-scatter.1
